TPU v7x, 128 devices: a whole 4x4x4 slice. The times are simulated.
128 devices in a mesh: section: 16 (over z, x), bond: 8 (over y, core).
Axes of the slice: x: 4, y: 4, z: 4, core: 2. Of those that a mesh axis runs over, the one named last changes fastest.
Arguments:
- site_tensor: float32 [16, 3072, 4, 3072], P('section', None, None, 'bond'), may hold values from -0.109375 to 0.109375
- boundary: float32 [128, 3072], replicated, may hold values from -6 to 6
- selected: int32 [16, 128], P('section'), may hold values from 0 to 3
Outputs:
- chosen_prob: float32 [16, 128], P('section')
- exit_rows: float32 [16, 128, 3072], P('section', None, 'bond')
All inputs are finite; a program needn't handle non-finite values.
Results may differ from a plain program's by a relative error of at most 0.0003.
Values sent between devices are 32-bit elements; how exact they have to be, the bound alone decides.
A program may use at most 128 MiB of HBM per device.

v0:
```python
import jax
import jax.numpy as jnp
from jax import lax
from jax.sharding import PartitionSpec as P

BATCH = 64


def from_behind(array, axis, by):
    count = lax.axis_size(axis)
    pairs = [(i, i + by) for i in range(count) if 0 <= i + by < count]
    return lax.ppermute(array, axis, pairs)


def finish(amplitudes, chosen, block_rows, outcomes, columns, width):
    shaped = amplitudes.reshape(block_rows, outcomes, columns)
    partial_weight = jnp.sum(shaped * shaped, axis=2)
    weight = lax.psum(partial_weight, "bond")
    outcome_ids = jnp.arange(outcomes, dtype=jnp.int32)
    onehot = (chosen[:, None] == outcome_ids[None, :]).astype(jnp.float32)
    chosen_weight = jnp.sum(onehot * weight, axis=1)
    prob_block = chosen_weight / jnp.sum(weight, axis=1)
    chosen_row = jnp.sum(onehot[:, :, None] * shaped, axis=1)
    next_block = chosen_row / jnp.sqrt(chosen_weight / width + 1e-06)[:, None]
    return (prob_block, next_block)


def on_device(site_tensor, boundary, selected):
    width = site_tensor.shape[1]
    outcomes = site_tensor.shape[2]
    columns = site_tensor.shape[3]
    site_matrix = site_tensor[0].reshape(width, outcomes * columns)
    sections = lax.axis_size("section")
    section_index = lax.axis_index("section")
    total_rows = boundary.shape[0]
    block_rows = BATCH
    micro_count = total_rows // block_rows
    picks = selected[0]
    start_rows = jnp.zeros((block_rows, width), jnp.float32)
    prob_init = jnp.zeros((total_rows,), jnp.float32)
    rows_init = jnp.zeros((total_rows, columns), jnp.float32)

    def advance(step_index, carry):
        incoming, prob_out, rows_out = carry
        micro = step_index - section_index
        valid = jnp.logical_and(micro >= 0, micro < micro_count)
        slot = jnp.clip(micro, 0, micro_count - 1)
        feed = jnp.clip(step_index, 0, micro_count - 1).astype(jnp.int32)
        fresh = lax.dynamic_slice_in_dim(boundary, feed * block_rows, block_rows, 0)
        chosen = lax.dynamic_slice_in_dim(picks, slot * block_rows, block_rows, 0)
        current = jnp.where(section_index == 0, fresh, incoming)
        amplitudes = jnp.dot(
            current,
            site_matrix,
            precision=lax.Precision.HIGHEST,
            preferred_element_type=jnp.float32,
        )
        prob_block, next_block = finish(amplitudes, chosen, block_rows, outcomes, columns, width)
        old_prob = lax.dynamic_slice_in_dim(prob_out, slot * block_rows, block_rows, 0)
        old_rows = lax.dynamic_slice_in_dim(rows_out, slot * block_rows, block_rows, 0)
        prob_out = lax.dynamic_update_slice_in_dim(
            prob_out, jnp.where(valid, prob_block, old_prob), slot * block_rows, 0
        )
        rows_out = lax.dynamic_update_slice_in_dim(
            rows_out, jnp.where(valid, next_block, old_rows), slot * block_rows, 0
        )
        whole_rows = lax.all_gather(next_block, "bond", axis=1, tiled=True)
        incoming = from_behind(whole_rows, "section", 1)
        return (incoming, prob_out, rows_out)

    final_carry = lax.fori_loop(
        0, micro_count + sections - 1, advance, (start_rows, prob_init, rows_init)
    )
    return (final_carry[1][None, :], final_carry[2][None, :, :])


def solution(mesh):
    in_specs = (P("section", None, None, "bond"), P(), P("section", None))
    out_specs = (P("section", None), P("section", None, "bond"))
    return jax.shard_map(
        on_device, mesh=mesh, in_specs=in_specs, out_specs=out_specs, check_vma=False
    )
```

profile of v0, /device:TPU:103, one launch (start us, length us, event | category | flops | bytes accessed | tf_op | source)
XLA Modules:
  0.0 1313.0 jit_solution(2115595274633260697)
XLA Ops:
  17.3 1295.1 %while.18 = (s32[]{:T(128)}, f32[64,3072]{1,0:T(8,128)S(1)}, f32[128]{0:T(128)S(1)}, f32[128,384]{1,0:T(8,128)S(1)}, s32[]{:T(128)}, /*index=5*/s32[128]{0:T(128...) while((s32[]{:T(128)}, f32[64,3072]{1,0:T(8,128)S(1)}, ...), condition=%wide.region_6.7_spmd, body=%wide.region_0.6_spmd.sunk | while | flops 3624494848 | bytes 26552424 | solution.py:71
  32.7 23.0 %psum.13 = f32[64,4]{1,0:T(8,128)S(1)} all-reduce(f32[64,4]{1,0:T(8,128)S(1)} %get-tuple-element.271), channel_id=1, replica_groups=mesh['section'=16,'bond'=8] {'bond'}, use_global_device_ids=true, to_apply=%region_3.3 | all-reduce | flops 256 | bytes 2048 | tf_op jit(solution)/shard_map/while/body/eval_jaxpr/psum | solution.py:18
  74.2 19.5 %collective-permute-done = f32[64,3072]{1,0:T(8,128)S(1)} collective-permute-done((f32[64,3072]{1,0:T(8,128)S(1)}, f32[64,3072]{1,0:T(8,128)S(1)}, u32[]{:S(2)}, u32[]{:S(2)}) %collective-permute-start) | collective-permute-done | bytes 786464 | tf_op jit(solution)/shard_map/while/body/eval_jaxpr/ppermute | solution.py:12
  109.1 21.1 %psum.13 = f32[64,4]{1,0:T(8,128)S(1)} all-reduce(f32[64,4]{1,0:T(8,128)S(1)} %get-tuple-element.271), channel_id=1, replica_groups=mesh['section'=16,'bond'=8] {'bond'}, use_global_device_ids=true, to_apply=%region_3.3 | all-reduce | flops 256 | bytes 2048 | tf_op jit(solution)/shard_map/while/body/eval_jaxpr/psum | solution.py:18
  183.6 21.1 %psum.13 = f32[64,4]{1,0:T(8,128)S(1)} all-reduce(f32[64,4]{1,0:T(8,128)S(1)} %get-tuple-element.271), channel_id=1, replica_groups=mesh['section'=16,'bond'=8] {'bond'}, use_global_device_ids=true, to_apply=%region_3.3 | all-reduce | flops 256 | bytes 2048 | tf_op jit(solution)/shard_map/while/body/eval_jaxpr/psum | solution.py:18
  258.1 21.1 %psum.13 = f32[64,4]{1,0:T(8,128)S(1)} all-reduce(f32[64,4]{1,0:T(8,128)S(1)} %get-tuple-element.271), channel_id=1, replica_groups=mesh['section'=16,'bond'=8] {'bond'}, use_global_device_ids=true, to_apply=%region_3.3 | all-reduce | flops 256 | bytes 2048 | tf_op jit(solution)/shard_map/while/body/eval_jaxpr/psum | solution.py:18
  332.6 21.1 %psum.13 = f32[64,4]{1,0:T(8,128)S(1)} all-reduce(f32[64,4]{1,0:T(8,128)S(1)} %get-tuple-element.271), channel_id=1, replica_groups=mesh['section'=16,'bond'=8] {'bond'}, use_global_device_ids=true, to_apply=%region_3.3 | all-reduce | flops 256 | bytes 2048 | tf_op jit(solution)/shard_map/while/body/eval_jaxpr/psum | solution.py:18
  372.2 20.7 %collective-permute-done = f32[64,3072]{1,0:T(8,128)S(1)} collective-permute-done((f32[64,3072]{1,0:T(8,128)S(1)}, f32[64,3072]{1,0:T(8,128)S(1)}, u32[]{:S(2)}, u32[]{:S(2)}) %collective-permute-start) | collective-permute-done | bytes 786464 | tf_op jit(solution)/shard_map/while/body/eval_jaxpr/ppermute | solution.py:12
  408.3 20.8 %psum.13 = f32[64,4]{1,0:T(8,128)S(1)} all-reduce(f32[64,4]{1,0:T(8,128)S(1)} %get-tuple-element.271), channel_id=1, replica_groups=mesh['section'=16,'bond'=8] {'bond'}, use_global_device_ids=true, to_apply=%region_3.3 | all-reduce | flops 256 | bytes 2048 | tf_op jit(solution)/shard_map/while/body/eval_jaxpr/psum | solution.py:18
  447.7 21.9 %collective-permute-done = f32[64,3072]{1,0:T(8,128)S(1)} collective-permute-done((f32[64,3072]{1,0:T(8,128)S(1)}, f32[64,3072]{1,0:T(8,128)S(1)}, u32[]{:S(2)}, u32[]{:S(2)}) %collective-permute-start) | collective-permute-done | bytes 786464 | tf_op jit(solution)/shard_map/while/body/eval_jaxpr/ppermute | solution.py:12
  485.0 20.8 %psum.13 = f32[64,4]{1,0:T(8,128)S(1)} all-reduce(f32[64,4]{1,0:T(8,128)S(1)} %get-tuple-element.271), channel_id=1, replica_groups=mesh['section'=16,'bond'=8] {'bond'}, use_global_device_ids=true, to_apply=%region_3.3 | all-reduce | flops 256 | bytes 2048 | tf_op jit(solution)/shard_map/while/body/eval_jaxpr/psum | solution.py:18
  524.3 21.9 %collective-permute-done = f32[64,3072]{1,0:T(8,128)S(1)} collective-permute-done((f32[64,3072]{1,0:T(8,128)S(1)}, f32[64,3072]{1,0:T(8,128)S(1)}, u32[]{:S(2)}, u32[]{:S(2)}) %collective-permute-start) | collective-permute-done | bytes 786464 | tf_op jit(solution)/shard_map/while/body/eval_jaxpr/ppermute | solution.py:12
  561.6 20.8 %psum.13 = f32[64,4]{1,0:T(8,128)S(1)} all-reduce(f32[64,4]{1,0:T(8,128)S(1)} %get-tuple-element.271), channel_id=1, replica_groups=mesh['section'=16,'bond'=8] {'bond'}, use_global_device_ids=true, to_apply=%region_3.3 | all-reduce | flops 256 | bytes 2048 | tf_op jit(solution)/shard_map/while/body/eval_jaxpr/psum | solution.py:18
  600.9 21.9 %collective-permute-done = f32[64,3072]{1,0:T(8,128)S(1)} collective-permute-done((f32[64,3072]{1,0:T(8,128)S(1)}, f32[64,3072]{1,0:T(8,128)S(1)}, u32[]{:S(2)}, u32[]{:S(2)}) %collective-permute-start) | collective-permute-done | bytes 786464 | tf_op jit(solution)/shard_map/while/body/eval_jaxpr/ppermute | solution.py:12
  638.2 20.8 %psum.13 = f32[64,4]{1,0:T(8,128)S(1)} all-reduce(f32[64,4]{1,0:T(8,128)S(1)} %get-tuple-element.271), channel_id=1, replica_groups=mesh['section'=16,'bond'=8] {'bond'}, use_global_device_ids=true, to_apply=%region_3.3 | all-reduce | flops 256 | bytes 2048 | tf_op jit(solution)/shard_map/while/body/eval_jaxpr/psum | solution.py:18
  677.5 21.9 %collective-permute-done = f32[64,3072]{1,0:T(8,128)S(1)} collective-permute-done((f32[64,3072]{1,0:T(8,128)S(1)}, f32[64,3072]{1,0:T(8,128)S(1)}, u32[]{:S(2)}, u32[]{:S(2)}) %collective-permute-start) | collective-permute-done | bytes 786464 | tf_op jit(solution)/shard_map/while/body/eval_jaxpr/ppermute | solution.py:12
  714.8 20.8 %psum.13 = f32[64,4]{1,0:T(8,128)S(1)} all-reduce(f32[64,4]{1,0:T(8,128)S(1)} %get-tuple-element.271), channel_id=1, replica_groups=mesh['section'=16,'bond'=8] {'bond'}, use_global_device_ids=true, to_apply=%region_3.3 | all-reduce | flops 256 | bytes 2048 | tf_op jit(solution)/shard_map/while/body/eval_jaxpr/psum | solution.py:18
  754.1 21.9 %collective-permute-done = f32[64,3072]{1,0:T(8,128)S(1)} collective-permute-done((f32[64,3072]{1,0:T(8,128)S(1)}, f32[64,3072]{1,0:T(8,128)S(1)}, u32[]{:S(2)}, u32[]{:S(2)}) %collective-permute-start) | collective-permute-done | bytes 786464 | tf_op jit(solution)/shard_map/while/body/eval_jaxpr/ppermute | solution.py:12
  791.4 20.8 %psum.13 = f32[64,4]{1,0:T(8,128)S(1)} all-reduce(f32[64,4]{1,0:T(8,128)S(1)} %get-tuple-element.271), channel_id=1, replica_groups=mesh['section'=16,'bond'=8] {'bond'}, use_global_device_ids=true, to_apply=%region_3.3 | all-reduce | flops 256 | bytes 2048 | tf_op jit(solution)/shard_map/while/body/eval_jaxpr/psum | solution.py:18
  830.7 21.9 %collective-permute-done = f32[64,3072]{1,0:T(8,128)S(1)} collective-permute-done((f32[64,3072]{1,0:T(8,128)S(1)}, f32[64,3072]{1,0:T(8,128)S(1)}, u32[]{:S(2)}, u32[]{:S(2)}) %collective-permute-start) | collective-permute-done | bytes 786464 | tf_op jit(solution)/shard_map/while/body/eval_jaxpr/ppermute | solution.py:12
  868.0 20.8 %psum.13 = f32[64,4]{1,0:T(8,128)S(1)} all-reduce(f32[64,4]{1,0:T(8,128)S(1)} %get-tuple-element.271), channel_id=1, replica_groups=mesh['section'=16,'bond'=8] {'bond'}, use_global_device_ids=true, to_apply=%region_3.3 | all-reduce | flops 256 | bytes 2048 | tf_op jit(solution)/shard_map/while/body/eval_jaxpr/psum | solution.py:18
  907.3 21.9 %collective-permute-done = f32[64,3072]{1,0:T(8,128)S(1)} collective-permute-done((f32[64,3072]{1,0:T(8,128)S(1)}, f32[64,3072]{1,0:T(8,128)S(1)}, u32[]{:S(2)}, u32[]{:S(2)}) %collective-permute-start) | collective-permute-done | bytes 786464 | tf_op jit(solution)/shard_map/while/body/eval_jaxpr/ppermute | solution.py:12
  944.6 20.8 %psum.13 = f32[64,4]{1,0:T(8,128)S(1)} all-reduce(f32[64,4]{1,0:T(8,128)S(1)} %get-tuple-element.271), channel_id=1, replica_groups=mesh['section'=16,'bond'=8] {'bond'}, use_global_device_ids=true, to_apply=%region_3.3 | all-reduce | flops 256 | bytes 2048 | tf_op jit(solution)/shard_map/while/body/eval_jaxpr/psum | solution.py:18
  984.0 21.9 %collective-permute-done = f32[64,3072]{1,0:T(8,128)S(1)} collective-permute-done((f32[64,3072]{1,0:T(8,128)S(1)}, f32[64,3072]{1,0:T(8,128)S(1)}, u32[]{:S(2)}, u32[]{:S(2)}) %collective-permute-start) | collective-permute-done | bytes 786464 | tf_op jit(solution)/shard_map/while/body/eval_jaxpr/ppermute | solution.py:12
  1021.3 20.8 %psum.13 = f32[64,4]{1,0:T(8,128)S(1)} all-reduce(f32[64,4]{1,0:T(8,128)S(1)} %get-tuple-element.271), channel_id=1, replica_groups=mesh['section'=16,'bond'=8] {'bond'}, use_global_device_ids=true, to_apply=%region_3.3 | all-reduce | flops 256 | bytes 2048 | tf_op jit(solution)/shard_map/while/body/eval_jaxpr/psum | solution.py:18
  1060.6 21.9 %collective-permute-done = f32[64,3072]{1,0:T(8,128)S(1)} collective-permute-done((f32[64,3072]{1,0:T(8,128)S(1)}, f32[64,3072]{1,0:T(8,128)S(1)}, u32[]{:S(2)}, u32[]{:S(2)}) %collective-permute-start) | collective-permute-done | bytes 786464 | tf_op jit(solution)/shard_map/while/body/eval_jaxpr/ppermute | solution.py:12
  1097.9 20.8 %psum.13 = f32[64,4]{1,0:T(8,128)S(1)} all-reduce(f32[64,4]{1,0:T(8,128)S(1)} %get-tuple-element.271), channel_id=1, replica_groups=mesh['section'=16,'bond'=8] {'bond'}, use_global_device_ids=true, to_apply=%region_3.3 | all-reduce | flops 256 | bytes 2048 | tf_op jit(solution)/shard_map/while/body/eval_jaxpr/psum | solution.py:18
  1137.2 21.9 %collective-permute-done = f32[64,3072]{1,0:T(8,128)S(1)} collective-permute-done((f32[64,3072]{1,0:T(8,128)S(1)}, f32[64,3072]{1,0:T(8,128)S(1)}, u32[]{:S(2)}, u32[]{:S(2)}) %collective-permute-start) | collective-permute-done | bytes 786464 | tf_op jit(solution)/shard_map/while/body/eval_jaxpr/ppermute | solution.py:12
  1174.5 20.8 %psum.13 = f32[64,4]{1,0:T(8,128)S(1)} all-reduce(f32[64,4]{1,0:T(8,128)S(1)} %get-tuple-element.271), channel_id=1, replica_groups=mesh['section'=16,'bond'=8] {'bond'}, use_global_device_ids=true, to_apply=%region_3.3 | all-reduce | flops 256 | bytes 2048 | tf_op jit(solution)/shard_map/while/body/eval_jaxpr/psum | solution.py:18
  1213.8 21.9 %collective-permute-done = f32[64,3072]{1,0:T(8,128)S(1)} collective-permute-done((f32[64,3072]{1,0:T(8,128)S(1)}, f32[64,3072]{1,0:T(8,128)S(1)}, u32[]{:S(2)}, u32[]{:S(2)}) %collective-permute-start) | collective-permute-done | bytes 786464 | tf_op jit(solution)/shard_map/while/body/eval_jaxpr/ppermute | solution.py:12
  1251.1 20.8 %psum.13 = f32[64,4]{1,0:T(8,128)S(1)} all-reduce(f32[64,4]{1,0:T(8,128)S(1)} %get-tuple-element.271), channel_id=1, replica_groups=mesh['section'=16,'bond'=8] {'bond'}, use_global_device_ids=true, to_apply=%region_3.3 | all-reduce | flops 256 | bytes 2048 | tf_op jit(solution)/shard_map/while/body/eval_jaxpr/psum | solution.py:18
  1290.4 21.9 %collective-permute-done = f32[64,3072]{1,0:T(8,128)S(1)} collective-permute-done((f32[64,3072]{1,0:T(8,128)S(1)}, f32[64,3072]{1,0:T(8,128)S(1)}, u32[]{:S(2)}, u32[]{:S(2)}) %collective-permute-start) | collective-permute-done | bytes 786464 | tf_op jit(solution)/shard_map/while/body/eval_jaxpr/ppermute | solution.py:12
  (185 shorter events, 651.2 us)
Async XLA Ops:
  0.6 16.6 %copy-start = (f32[128,3072]{1,0:T(8,128)S(1)}, f32[128,3072]{1,0:T(8,128)}, u32[]{:S(2)}) copy-start(f32[128,3072]{1,0:T(8,128)} %param.6) | copy-start | bytes 4718596
  0.6 16.6 %copy-start.3 = (s32[1,128]{1,0:T(1,128)S(1)}, s32[1,128]{1,0:T(1,128)}, u32[]{:S(2)}) copy-start(s32[1,128]{1,0:T(1,128)} %param.7) | copy-start | bytes 1540
  72.9 20.8 %collective-permute-start = (f32[64,3072]{1,0:T(8,128)S(1)}, f32[64,3072]{1,0:T(8,128)S(1)}, u32[]{:S(2)}, u32[]{:S(2)}) collective-permute-start(f32[64,3072]{1,0:T(8,128)S(1)} %all_gather.9), channel_id=1, source_target_pairs={{0,8},{8,16},{16,24},{24,32},{32,40},{40,48},{48,56},{56,64},{64,7... | collective-permute-start | bytes 2359304 | tf_op jit(solution)/shard_map/while/body/eval_jaxpr/ppermute | solution.py:12
  147.4 20.8 %collective-permute-start = (f32[64,3072]{1,0:T(8,128)S(1)}, f32[64,3072]{1,0:T(8,128)S(1)}, u32[]{:S(2)}, u32[]{:S(2)}) collective-permute-start(f32[64,3072]{1,0:T(8,128)S(1)} %all_gather.9), channel_id=1, source_target_pairs={{0,8},{8,16},{16,24},{24,32},{32,40},{40,48},{48,56},{56,64},{64,7... | collective-permute-start | bytes 2359304 | tf_op jit(solution)/shard_map/while/body/eval_jaxpr/ppermute | solution.py:12
  221.9 20.8 %collective-permute-start = (f32[64,3072]{1,0:T(8,128)S(1)}, f32[64,3072]{1,0:T(8,128)S(1)}, u32[]{:S(2)}, u32[]{:S(2)}) collective-permute-start(f32[64,3072]{1,0:T(8,128)S(1)} %all_gather.9), channel_id=1, source_target_pairs={{0,8},{8,16},{16,24},{24,32},{32,40},{40,48},{48,56},{56,64},{64,7... | collective-permute-start | bytes 2359304 | tf_op jit(solution)/shard_map/while/body/eval_jaxpr/ppermute | solution.py:12
  296.4 20.8 %collective-permute-start = (f32[64,3072]{1,0:T(8,128)S(1)}, f32[64,3072]{1,0:T(8,128)S(1)}, u32[]{:S(2)}, u32[]{:S(2)}) collective-permute-start(f32[64,3072]{1,0:T(8,128)S(1)} %all_gather.9), channel_id=1, source_target_pairs={{0,8},{8,16},{16,24},{24,32},{32,40},{40,48},{48,56},{56,64},{64,7... | collective-permute-start | bytes 2359304 | tf_op jit(solution)/shard_map/while/body/eval_jaxpr/ppermute | solution.py:12
  370.9 22.0 %collective-permute-start = (f32[64,3072]{1,0:T(8,128)S(1)}, f32[64,3072]{1,0:T(8,128)S(1)}, u32[]{:S(2)}, u32[]{:S(2)}) collective-permute-start(f32[64,3072]{1,0:T(8,128)S(1)} %all_gather.9), channel_id=1, source_target_pairs={{0,8},{8,16},{16,24},{24,32},{32,40},{40,48},{48,56},{56,64},{64,7... | collective-permute-start | bytes 2359304 | tf_op jit(solution)/shard_map/while/body/eval_jaxpr/ppermute | solution.py:12
  446.4 23.2 %collective-permute-start = (f32[64,3072]{1,0:T(8,128)S(1)}, f32[64,3072]{1,0:T(8,128)S(1)}, u32[]{:S(2)}, u32[]{:S(2)}) collective-permute-start(f32[64,3072]{1,0:T(8,128)S(1)} %all_gather.9), channel_id=1, source_target_pairs={{0,8},{8,16},{16,24},{24,32},{32,40},{40,48},{48,56},{56,64},{64,7... | collective-permute-start | bytes 2359304 | tf_op jit(solution)/shard_map/while/body/eval_jaxpr/ppermute | solution.py:12
  523.0 23.2 %collective-permute-start = (f32[64,3072]{1,0:T(8,128)S(1)}, f32[64,3072]{1,0:T(8,128)S(1)}, u32[]{:S(2)}, u32[]{:S(2)}) collective-permute-start(f32[64,3072]{1,0:T(8,128)S(1)} %all_gather.9), channel_id=1, source_target_pairs={{0,8},{8,16},{16,24},{24,32},{32,40},{40,48},{48,56},{56,64},{64,7... | collective-permute-start | bytes 2359304 | tf_op jit(solution)/shard_map/while/body/eval_jaxpr/ppermute | solution.py:12
  599.6 23.2 %collective-permute-start = (f32[64,3072]{1,0:T(8,128)S(1)}, f32[64,3072]{1,0:T(8,128)S(1)}, u32[]{:S(2)}, u32[]{:S(2)}) collective-permute-start(f32[64,3072]{1,0:T(8,128)S(1)} %all_gather.9), channel_id=1, source_target_pairs={{0,8},{8,16},{16,24},{24,32},{32,40},{40,48},{48,56},{56,64},{64,7... | collective-permute-start | bytes 2359304 | tf_op jit(solution)/shard_map/while/body/eval_jaxpr/ppermute | solution.py:12
  676.2 23.2 %collective-permute-start = (f32[64,3072]{1,0:T(8,128)S(1)}, f32[64,3072]{1,0:T(8,128)S(1)}, u32[]{:S(2)}, u32[]{:S(2)}) collective-permute-start(f32[64,3072]{1,0:T(8,128)S(1)} %all_gather.9), channel_id=1, source_target_pairs={{0,8},{8,16},{16,24},{24,32},{32,40},{40,48},{48,56},{56,64},{64,7... | collective-permute-start | bytes 2359304 | tf_op jit(solution)/shard_map/while/body/eval_jaxpr/ppermute | solution.py:12
  752.8 23.2 %collective-permute-start = (f32[64,3072]{1,0:T(8,128)S(1)}, f32[64,3072]{1,0:T(8,128)S(1)}, u32[]{:S(2)}, u32[]{:S(2)}) collective-permute-start(f32[64,3072]{1,0:T(8,128)S(1)} %all_gather.9), channel_id=1, source_target_pairs={{0,8},{8,16},{16,24},{24,32},{32,40},{40,48},{48,56},{56,64},{64,7... | collective-permute-start | bytes 2359304 | tf_op jit(solution)/shard_map/while/body/eval_jaxpr/ppermute | solution.py:12
  829.4 23.2 %collective-permute-start = (f32[64,3072]{1,0:T(8,128)S(1)}, f32[64,3072]{1,0:T(8,128)S(1)}, u32[]{:S(2)}, u32[]{:S(2)}) collective-permute-start(f32[64,3072]{1,0:T(8,128)S(1)} %all_gather.9), channel_id=1, source_target_pairs={{0,8},{8,16},{16,24},{24,32},{32,40},{40,48},{48,56},{56,64},{64,7... | collective-permute-start | bytes 2359304 | tf_op jit(solution)/shard_map/while/body/eval_jaxpr/ppermute | solution.py:12
  906.1 23.2 %collective-permute-start = (f32[64,3072]{1,0:T(8,128)S(1)}, f32[64,3072]{1,0:T(8,128)S(1)}, u32[]{:S(2)}, u32[]{:S(2)}) collective-permute-start(f32[64,3072]{1,0:T(8,128)S(1)} %all_gather.9), channel_id=1, source_target_pairs={{0,8},{8,16},{16,24},{24,32},{32,40},{40,48},{48,56},{56,64},{64,7... | collective-permute-start | bytes 2359304 | tf_op jit(solution)/shard_map/while/body/eval_jaxpr/ppermute | solution.py:12
  982.7 23.2 %collective-permute-start = (f32[64,3072]{1,0:T(8,128)S(1)}, f32[64,3072]{1,0:T(8,128)S(1)}, u32[]{:S(2)}, u32[]{:S(2)}) collective-permute-start(f32[64,3072]{1,0:T(8,128)S(1)} %all_gather.9), channel_id=1, source_target_pairs={{0,8},{8,16},{16,24},{24,32},{32,40},{40,48},{48,56},{56,64},{64,7... | collective-permute-start | bytes 2359304 | tf_op jit(solution)/shard_map/while/body/eval_jaxpr/ppermute | solution.py:12
  1059.3 23.2 %collective-permute-start = (f32[64,3072]{1,0:T(8,128)S(1)}, f32[64,3072]{1,0:T(8,128)S(1)}, u32[]{:S(2)}, u32[]{:S(2)}) collective-permute-start(f32[64,3072]{1,0:T(8,128)S(1)} %all_gather.9), channel_id=1, source_target_pairs={{0,8},{8,16},{16,24},{24,32},{32,40},{40,48},{48,56},{56,64},{64,7... | collective-permute-start | bytes 2359304 | tf_op jit(solution)/shard_map/while/body/eval_jaxpr/ppermute | solution.py:12
  1135.9 23.2 %collective-permute-start = (f32[64,3072]{1,0:T(8,128)S(1)}, f32[64,3072]{1,0:T(8,128)S(1)}, u32[]{:S(2)}, u32[]{:S(2)}) collective-permute-start(f32[64,3072]{1,0:T(8,128)S(1)} %all_gather.9), channel_id=1, source_target_pairs={{0,8},{8,16},{16,24},{24,32},{32,40},{40,48},{48,56},{56,64},{64,7... | collective-permute-start | bytes 2359304 | tf_op jit(solution)/shard_map/while/body/eval_jaxpr/ppermute | solution.py:12
  1212.5 23.2 %collective-permute-start = (f32[64,3072]{1,0:T(8,128)S(1)}, f32[64,3072]{1,0:T(8,128)S(1)}, u32[]{:S(2)}, u32[]{:S(2)}) collective-permute-start(f32[64,3072]{1,0:T(8,128)S(1)} %all_gather.9), channel_id=1, source_target_pairs={{0,8},{8,16},{16,24},{24,32},{32,40},{40,48},{48,56},{56,64},{64,7... | collective-permute-start | bytes 2359304 | tf_op jit(solution)/shard_map/while/body/eval_jaxpr/ppermute | solution.py:12
  1289.1 23.2 %collective-permute-start = (f32[64,3072]{1,0:T(8,128)S(1)}, f32[64,3072]{1,0:T(8,128)S(1)}, u32[]{:S(2)}, u32[]{:S(2)}) collective-permute-start(f32[64,3072]{1,0:T(8,128)S(1)} %all_gather.9), channel_id=1, source_target_pairs={{0,8},{8,16},{16,24},{24,32},{32,40},{40,48},{48,56},{56,64},{64,7... | collective-permute-start | bytes 2359304 | tf_op jit(solution)/shard_map/while/body/eval_jaxpr/ppermute | solution.py:12
  1312.3 0.7 copy-start.1
  1312.3 0.7 copy-start.2
where the time goes:
time: 1320 us; the launch traced here: 1310 us
  blocking collectives  642 us (49%)
  waiting for transfers between devices  362 us (27%)
  matrix products  249 us (19%)
  starting transfers between devices  21.8 us (2%)
  local copies, waits for them, and re-layouts  20.8 us (2%)
  other arithmetic  16.1 us (1%)
    ppermute x17, waiting for transfers between devices, from_behind(): return lax.ppermute(array, axis, pairs)  362 us
    psum x17, blocking collectives, finish(): weight = lax.psum(partial_weight, 'bond')  357 us
    all_gather x17, blocking collectives, advance(): whole_rows = lax.all_gather(next_block, 'bond', axis=1, tiled=True)  285 us
    dot_general x17, matrix products, advance(): jnp.dot(current, site_matrix, precision=lax.Precision.HIGHEST, preferred_...  249 us
  transfers between devices with their start and end apart: 17, of which 17 were waited for; matrix products, arithmetic and copies ran while one was open for 0% of the time, Pallas kernels for 0%

commit v1 on v0

v1 whole, which is shorter than its diff:
```python
import functools

import jax
import jax.numpy as jnp
from jax import lax
from jax.experimental import pallas as pl
from jax.experimental.pallas import tpu as pltpu
from jax.sharding import PartitionSpec as P

MESH = pl.DeviceIdType.MESH
BATCH = 8
FILL = 192
SLOTS = 4
DIRECT = ((1, 0), (1, 1), (2, 0), (2, 1), (3, 0), (3, 1), (0, 0), (0, 1))
ORDER = (3, 0, 1, 2)


def kernel(
    sel_ref, w_hbm, start_hbm, prob_ref, rows_ref,
    stage, whi, wlo, left, chosen_rows, acc, picks, part, totals, inverse,
    fill_sem, start_sem, send_sem, recv_sem, wsend_sem, wrecv_sem,
):
    rows, width = left.shape
    outcomes, columns = w_hbm.shape[2], w_hbm.shape[3]
    sections, peers = lax.axis_size("section"), lax.axis_size("bond")
    chips = peers // 2
    batches = rows // BATCH
    fills = width // FILL
    section, me = lax.axis_index("section"), lax.axis_index("bond")
    y, core = me // 2, lax.rem(me, 2)
    following = lax.rem(section + 1, sections)
    before = lax.rem(section + sections - 1, sections)
    first, last = section == 0, section == sections - 1

    def fill(step):
        slot = lax.rem(step, SLOTS)
        return pltpu.make_async_copy(
            w_hbm.at[0, pl.ds(step * FILL, FILL)], stage.at[slot], fill_sem.at[slot]
        )

    for step in range(SLOTS):
        fill(step).start()

    @pl.when(first)
    def _():
        pltpu.make_async_copy(start_hbm, left, start_sem).start()

    barrier = pltpu.get_barrier_semaphore()
    for peer in range(peers):
        for other in (before, following):
            pl.semaphore_signal(barrier, inc=1, device_id=(other, peer), device_id_type=MESH)
    for ahead in range(1, peers):
        pl.semaphore_signal(
            barrier, inc=1, device_id=(section, lax.rem(me + ahead, peers)), device_id_type=MESH
        )

    picks[...] = jnp.broadcast_to(sel_ref[...].astype(jnp.float32), (rows, rows)).T

    def split(step, _):
        slot = lax.rem(step, SLOTS)
        fill(step).wait()

        def some(piece, _):
            row = pl.multiple_of(piece * 32, 32)
            for k in range(outcomes):
                whole = stage[slot, pl.ds(row, 32), k, :]
                high = whole.astype(jnp.bfloat16)
                low = (whole - high.astype(jnp.float32)).astype(jnp.bfloat16)
                at = pl.ds(pl.multiple_of(step * FILL + row, 32), 32)
                whi[at, k * columns : (k + 1) * columns] = high
                wlo[at, k * columns : (k + 1) * columns] = low
            return 0

        lax.fori_loop(0, FILL // 32, some, 0)

        @pl.when(step + SLOTS < fills)
        def _():
            fill(step + SLOTS).start()

        return 0

    lax.fori_loop(0, fills, split, 0)

    pl.semaphore_wait(barrier, 3 * peers - 1)

    @pl.when(first)
    def _():
        pltpu.make_async_copy(start_hbm, left, start_sem).wait()

    def send(batch, index):
        ahead, other = DIRECT[index]
        peer = lax.rem(y + ahead, chips) * 2 + (lax.rem(core + 1, 2) if other else core)
        at = pl.ds(pl.multiple_of(batch * BATCH, BATCH), BATCH)
        return pltpu.make_async_remote_copy(
            src_ref=chosen_rows.at[at],
            dst_ref=left.at[at, pl.ds(pl.multiple_of(me * columns, columns), columns)],
            send_sem=send_sem.at[batch, index],
            recv_sem=recv_sem.at[batch, y],
            device_id=(following, peer),
            device_id_type=MESH,
        )

    lanes = lax.broadcasted_iota(jnp.int32, (BATCH, rows), 1)

    def advance(batch, _):
        at = pl.ds(pl.multiple_of(batch * BATCH, BATCH), BATCH)
        square = jnp.zeros((BATCH, 128), jnp.float32)
        for count, ahead in enumerate(ORDER):
            chip = lax.rem(y + ahead, chips)
            span = pl.ds(pl.multiple_of(chip * 2 * columns, 2 * columns), 2 * columns)

            @pl.when(jnp.logical_not(first))
            def _():
                pltpu.make_async_copy(left.at[at, span], left.at[at, span], recv_sem.at[batch, chip]).wait()

            x = left[at, span]
            high = x.astype(jnp.bfloat16).astype(jnp.float32)
            both = jnp.concatenate([high, x - high], axis=0).astype(jnp.bfloat16)
            for lane in range(2 * columns // 128):
                piece = x[:, lane * 128 : (lane + 1) * 128]
                square += piece * piece
            product = jnp.dot(both, whi[span, :], preferred_element_type=jnp.float32) + jnp.dot(
                both, wlo[span, :], preferred_element_type=jnp.float32
            )
            product = product[:BATCH] + product[BATCH:]
            if count == 0:
                acc[...] = product
            else:
                acc[...] += product
        norm = jnp.sum(square, axis=1, keepdims=True) / width
        scale = jnp.where(first, 1.0, 1.0 / jnp.sqrt(norm + 1e-06))
        chosen = jnp.zeros((BATCH, columns), jnp.float32)
        weight = jnp.zeros((BATCH, rows), jnp.float32)
        pick = picks[at, 0:1]
        amplitudes = []
        for k in range(outcomes):
            amplitude = acc[:, k * columns : (k + 1) * columns] * scale
            amplitudes.append(amplitude)
            chosen += jnp.where(pick == k, amplitude, 0.0)
        chosen_rows[at, :] = chosen

        @pl.when(jnp.logical_not(last))
        def _():
            for index in range(len(DIRECT)):
                send(batch, index).start()

        for k, amplitude in enumerate(amplitudes):
            squared = jnp.sum(amplitude * amplitude, axis=1, keepdims=True)
            weight += jnp.where(lanes == k, squared, 0.0)
        part[at, :] = weight
        return 0

    lax.fori_loop(0, batches, advance, 0)

    totals[me] = part[...].T[:8]

    def share(ahead):
        return pltpu.make_async_remote_copy(
            src_ref=totals.at[me],
            dst_ref=totals.at[me],
            send_sem=wsend_sem.at[ahead],
            recv_sem=wrecv_sem.at[ahead],
            device_id=(section, lax.rem(me + ahead, peers)),
            device_id_type=MESH,
        )

    for ahead in range(1, peers):
        share(ahead).start()
    for ahead in range(1, peers):
        share(ahead).wait_recv()
    total = totals[0]
    for peer in range(1, peers):
        total += totals[peer]
    whole = jnp.zeros((1, rows), jnp.float32)
    taken = jnp.zeros((1, rows), jnp.float32)
    for k in range(outcomes):
        whole += total[k : k + 1]
        taken += jnp.where(sel_ref[...] == k, total[k : k + 1], 0.0)
    prob_ref[...] = taken / whole
    divisor = jnp.sqrt(taken / width + 1e-06)
    inverse[...] = jnp.broadcast_to(divisor, (rows, rows)).T
    rows_ref[...] = chosen_rows[...] / inverse[:, 0:1]

    for ahead in range(1, peers):
        share(ahead).wait_send()

    @pl.when(jnp.logical_not(last))
    def _():
        def drain(batch, _):
            for index in range(len(DIRECT)):
                send(batch, index).wait_send()
            return 0

        lax.fori_loop(0, batches, drain, 0)


def on_device(site_tensor, boundary, selected):
    _, width, outcomes, columns = site_tensor.shape
    rows = boundary.shape[0]
    peers = lax.axis_size("bond")
    batches = rows // BATCH
    prob, out = pl.pallas_call(
        kernel,
        out_shape=(
            jax.ShapeDtypeStruct((1, rows), jnp.float32),
            jax.ShapeDtypeStruct((rows, columns), jnp.float32),
        ),
        in_specs=[
            pl.BlockSpec(memory_space=pltpu.VMEM),
            pl.BlockSpec(memory_space=pl.ANY),
            pl.BlockSpec(memory_space=pl.ANY),
        ],
        out_specs=(pl.BlockSpec(memory_space=pltpu.VMEM), pl.BlockSpec(memory_space=pltpu.VMEM)),
        scratch_shapes=[
            pltpu.VMEM((SLOTS, FILL, outcomes, columns), jnp.float32),
            pltpu.VMEM((width, outcomes * columns), jnp.bfloat16),
            pltpu.VMEM((width, outcomes * columns), jnp.bfloat16),
            pltpu.VMEM((rows, width), jnp.float32),
            pltpu.VMEM((rows, columns), jnp.float32),
            pltpu.VMEM((BATCH, outcomes * columns), jnp.float32),
            pltpu.VMEM((rows, rows), jnp.float32),
            pltpu.VMEM((rows, rows), jnp.float32),
            pltpu.VMEM((peers, 8, rows), jnp.float32),
            pltpu.VMEM((rows, rows), jnp.float32),
            pltpu.SemaphoreType.DMA((SLOTS,)),
            pltpu.SemaphoreType.DMA,
            pltpu.SemaphoreType.DMA((batches, len(DIRECT))),
            pltpu.SemaphoreType.DMA((batches, peers // 2)),
            pltpu.SemaphoreType.DMA((peers,)),
            pltpu.SemaphoreType.DMA((peers,)),
        ],
        compiler_params=pltpu.CompilerParams(
            collective_id=0, has_side_effects=True, vmem_limit_bytes=60 * 2**20
        ),
    )(selected, site_tensor, boundary)
    return prob, out[None]


def solution(mesh):
    in_specs = (P("section", None, None, "bond"), P(), P("section", None))
    out_specs = (P("section", None), P("section", None, "bond"))
    return jax.shard_map(
        on_device, mesh=mesh, in_specs=in_specs, out_specs=out_specs, check_vma=False
    )
```

time: 1320 us -> 218 us (0.17)
  blocking collectives: 642 us -> 0 us
  waiting for transfers between devices: 362 us -> 0 us
  matrix products: 249 us -> 0 us
  Pallas kernels: 0 us -> 214 us
  starting transfers between devices: 21.8 us -> 0 us
  local copies, waits for them, and re-layouts: 20.8 us -> 2.75 us
  other arithmetic: 16.1 us -> 0 us
    ppermute x17 -> x0, waiting for transfers between devices: 362 us -> none  [from_behind(): return lax.ppermute(array, axis, pairs)]
    psum x17 -> x0, blocking collectives: 357 us -> none  [finish(): weight = lax.psum(partial_weight, 'bond')]
    all_gather x17 -> x0, blocking collectives: 285 us -> none  [advance(): whole_rows = lax.all_gather(next_block, 'bond', axis=1, tiled=True)]
    dot_general x17 -> x0, matrix products: 249 us -> none  [advance(): jnp.dot(current, site_matrix, precision=lax.Precision.HIGHEST, preferred_...]
    pallas_call x0 -> x1, Pallas kernels: none -> 214 us  [on_device(): pl.pallas_call(kernel, out_shape=(jax.ShapeDtypeStruct((1, rows), jnp.flo...]
    ppermute x17 -> x0, starting transfers between devices: 21.8 us -> none  [from_behind(): return lax.ppermute(array, axis, pairs)]
    unnamed x9 -> x2, local copies, waits for them, and re-layouts: 17.2 us -> 2.75 us
  transfers between devices with their start and end apart: 17 -> 0, of which waited for: 17 -> 0; matrix products, arithmetic and copies ran while one was open for 0% -> 0% of each run, Pallas kernels for 0% -> 0%
where the time goes in v1:
time: 218 us
  Pallas kernels  214 us (98%)
  local copies, waits for them, and re-layouts  2.75 us (1%)
    pallas_call x1, Pallas kernels, on_device(): pl.pallas_call(kernel, out_shape=(jax.ShapeDtypeStruct((1, rows), jnp.flo...  214 us

profile of v1, /device:TPU:103, one launch (start us, length us, event | category | flops | bytes accessed | tf_op | source)
XLA Modules:
  0.0 217.8 jit_solution(11408642106601051238)
XLA Ops:
  0.6 214.4 %shard_map.50 = (f32[1,128]{1,0:T(1,128)}, f32[128,384]{1,0:T(8,128)}) custom-call(s32[1,128]{1,0:T(1,128)} %sel_ref.1, f32[1,3072,4,384]{3,2,1,0:T(4,128)} %w_hbm.1, f32[128,3072]{1,0:T(8,128)} %start_hbm.1), custom_call_target="tpu_custom_call" | custom-call | tf_op jit(solution)/shard_map/pallas_call | solution.py:202
  215.0 1.1 copy.7
  216.2 1.6 copy.8

commit v2 on v1

--- a/solution.py
+++ b/solution.py
@@ -8,17 +8,18 @@
 from jax.sharding import PartitionSpec as P
 
 MESH = pl.DeviceIdType.MESH
-BATCH = 8
+BATCH = 16
 FILL = 192
 SLOTS = 4
-DIRECT = ((1, 0), (1, 1), (2, 0), (2, 1), (3, 0), (3, 1), (0, 0), (0, 1))
-ORDER = (3, 0, 1, 2)
+SENDS = (0, 2, 1, 3)
+OWN, PASS, OTHER, PAIR = range(4)
+STEPS = ((0, OWN), (3, OWN), (0, OTHER), (2, OWN), (1, OWN), (3, OTHER), (2, OTHER), (1, OTHER))
 
 
 def kernel(
     sel_ref, w_hbm, start_hbm, prob_ref, rows_ref,
     stage, whi, wlo, left, chosen_rows, acc, picks, part, totals, inverse,
-    fill_sem, start_sem, send_sem, recv_sem, wsend_sem, wrecv_sem,
+    fill_sem, start_sem, send_sem, pass_sem, recv_sem, wsend_sem, wrecv_sem,
 ):
     rows, width = left.shape
     outcomes, columns = w_hbm.shape[2], w_hbm.shape[3]
@@ -32,14 +33,15 @@
     before = lax.rem(section + sections - 1, sections)
     first, last = section == 0, section == sections - 1
 
-    def fill(step):
+    def fill(step, k):
         slot = lax.rem(step, SLOTS)
         return pltpu.make_async_copy(
-            w_hbm.at[0, pl.ds(step * FILL, FILL)], stage.at[slot], fill_sem.at[slot]
+            w_hbm.at[0, pl.ds(step * FILL, FILL), k, :], stage.at[slot, k], fill_sem.at[slot, k]
         )
 
     for step in range(SLOTS):
-        fill(step).start()
+        for k in range(outcomes):
+            fill(step, k).start()
 
     @pl.when(first)
     def _():
@@ -58,12 +60,13 @@
 
     def split(step, _):
         slot = lax.rem(step, SLOTS)
-        fill(step).wait()
+        for k in range(outcomes):
+            fill(step, k).wait()
 
         def some(piece, _):
             row = pl.multiple_of(piece * 32, 32)
             for k in range(outcomes):
-                whole = stage[slot, pl.ds(row, 32), k, :]
+                whole = stage[slot, k, pl.ds(row, 32), :]
                 high = whole.astype(jnp.bfloat16)
                 low = (whole - high.astype(jnp.float32)).astype(jnp.bfloat16)
                 at = pl.ds(pl.multiple_of(step * FILL + row, 32), 32)
@@ -75,7 +78,8 @@
 
         @pl.when(step + SLOTS < fills)
         def _():
-            fill(step + SLOTS).start()
+            for k in range(outcomes):
+                fill(step + SLOTS, k).start()
 
         return 0
 
@@ -87,46 +91,71 @@
     def _():
         pltpu.make_async_copy(start_hbm, left, start_sem).wait()
 
+    def rows_of(batch):
+        return pl.ds(pl.multiple_of(batch * BATCH, BATCH), BATCH)
+
+    def block_of(source, count=1):
+        return pl.ds(pl.multiple_of(source * columns, columns), count * columns)
+
     def send(batch, index):
-        ahead, other = DIRECT[index]
-        peer = lax.rem(y + ahead, chips) * 2 + (lax.rem(core + 1, 2) if other else core)
-        at = pl.ds(pl.multiple_of(batch * BATCH, BATCH), BATCH)
+        at = rows_of(batch)
         return pltpu.make_async_remote_copy(
             src_ref=chosen_rows.at[at],
-            dst_ref=left.at[at, pl.ds(pl.multiple_of(me * columns, columns), columns)],
+            dst_ref=left.at[at, block_of(me)],
             send_sem=send_sem.at[batch, index],
-            recv_sem=recv_sem.at[batch, y],
-            device_id=(following, peer),
+            recv_sem=recv_sem.at[batch, me],
+            device_id=(following, lax.rem(y + SENDS[index], chips) * 2 + core),
             device_id_type=MESH,
         )
 
+    def relay(batch, source):
+        block = left.at[rows_of(batch), block_of(source)]
+        return pltpu.make_async_remote_copy(
+            src_ref=block,
+            dst_ref=block,
+            send_sem=pass_sem.at[batch, source // 2],
+            recv_sem=recv_sem.at[batch, source],
+            device_id=(section, y * 2 + 1 - core),
+            device_id_type=MESH,
+        )
+
+    def arrive(batch, source):
+        block = left.at[rows_of(batch), block_of(source)]
+        pltpu.make_async_copy(block, block, recv_sem.at[batch, source]).wait()
+
     lanes = lax.broadcasted_iota(jnp.int32, (BATCH, rows), 1)
 
     def advance(batch, _):
-        at = pl.ds(pl.multiple_of(batch * BATCH, BATCH), BATCH)
+        at = rows_of(batch)
         square = jnp.zeros((BATCH, 128), jnp.float32)
-        for count, ahead in enumerate(ORDER):
+        fresh = True
+        for ahead, what in STEPS:
             chip = lax.rem(y + ahead, chips)
-            span = pl.ds(pl.multiple_of(chip * 2 * columns, 2 * columns), 2 * columns)
+            source = chip * 2 + (core if what in (OWN, PASS) else 1 - core)
 
             @pl.when(jnp.logical_not(first))
             def _():
-                pltpu.make_async_copy(left.at[at, span], left.at[at, span], recv_sem.at[batch, chip]).wait()
-
+                arrive(batch, source)
+                if what in (OWN, PASS):
+                    relay(batch, source).start()
+
+            if what == PASS:
+                continue
+            span = block_of(chip * 2, 2) if what == PAIR else block_of(source)
             x = left[at, span]
             high = x.astype(jnp.bfloat16).astype(jnp.float32)
             both = jnp.concatenate([high, x - high], axis=0).astype(jnp.bfloat16)
-            for lane in range(2 * columns // 128):
+            for lane in range(x.shape[1] // 128):
                 piece = x[:, lane * 128 : (lane + 1) * 128]
                 square += piece * piece
-            product = jnp.dot(both, whi[span, :], preferred_element_type=jnp.float32) + jnp.dot(
-                both, wlo[span, :], preferred_element_type=jnp.float32
-            )
+            product = jnp.dot(both, whi[span, :], preferred_element_type=jnp.float32)
             product = product[:BATCH] + product[BATCH:]
-            if count == 0:
+            product += jnp.dot(both[:BATCH], wlo[span, :], preferred_element_type=jnp.float32)
+            if fresh:
                 acc[...] = product
             else:
                 acc[...] += product
+            fresh = False
         norm = jnp.sum(square, axis=1, keepdims=True) / width
         scale = jnp.where(first, 1.0, 1.0 / jnp.sqrt(norm + 1e-06))
         chosen = jnp.zeros((BATCH, columns), jnp.float32)
@@ -141,7 +170,7 @@
 
         @pl.when(jnp.logical_not(last))
         def _():
-            for index in range(len(DIRECT)):
+            for index in range(len(SENDS)):
                 send(batch, index).start()
 
         for k, amplitude in enumerate(amplitudes):
@@ -184,14 +213,20 @@
     for ahead in range(1, peers):
         share(ahead).wait_send()
 
-    @pl.when(jnp.logical_not(last))
-    def _():
-        def drain(batch, _):
-            for index in range(len(DIRECT)):
+    def drain(batch, _):
+        @pl.when(jnp.logical_not(last))
+        def _():
+            for index in range(len(SENDS)):
                 send(batch, index).wait_send()
-            return 0
-
-        lax.fori_loop(0, batches, drain, 0)
+
+        @pl.when(jnp.logical_not(first))
+        def _():
+            for chip in range(peers // 2):
+                relay(batch, chip * 2 + core).wait_send()
+
+        return 0
+
+    lax.fori_loop(0, batches, drain, 0)
 
 
 def on_device(site_tensor, boundary, selected):
@@ -212,7 +247,7 @@
         ],
         out_specs=(pl.BlockSpec(memory_space=pltpu.VMEM), pl.BlockSpec(memory_space=pltpu.VMEM)),
         scratch_shapes=[
-            pltpu.VMEM((SLOTS, FILL, outcomes, columns), jnp.float32),
+            pltpu.VMEM((SLOTS, outcomes, FILL, columns), jnp.float32),
             pltpu.VMEM((width, outcomes * columns), jnp.bfloat16),
             pltpu.VMEM((width, outcomes * columns), jnp.bfloat16),
             pltpu.VMEM((rows, width), jnp.float32),
@@ -222,10 +257,11 @@
             pltpu.VMEM((rows, rows), jnp.float32),
             pltpu.VMEM((peers, 8, rows), jnp.float32),
             pltpu.VMEM((rows, rows), jnp.float32),
-            pltpu.SemaphoreType.DMA((SLOTS,)),
+            pltpu.SemaphoreType.DMA((SLOTS, outcomes)),
             pltpu.SemaphoreType.DMA,
-            pltpu.SemaphoreType.DMA((batches, len(DIRECT))),
+            pltpu.SemaphoreType.DMA((batches, len(SENDS))),
             pltpu.SemaphoreType.DMA((batches, peers // 2)),
+            pltpu.SemaphoreType.DMA((batches, peers)),
             pltpu.SemaphoreType.DMA((peers,)),
             pltpu.SemaphoreType.DMA((peers,)),
         ],

time: 218 us -> 151 us (0.69)
  Pallas kernels: 214 us -> 148 us
    pallas_call x1, Pallas kernels: 214 us -> 148 us  [on_device(): pl.pallas_call(kernel, out_shape=(jax.ShapeDtypeStruct((1, rows), jnp.flo...]
where the time goes in v2:
time: 151 us
  Pallas kernels  148 us (98%)
  local copies, waits for them, and re-layouts  2.75 us (2%)
    pallas_call x1, Pallas kernels, on_device(): pl.pallas_call(kernel, out_shape=(jax.ShapeDtypeStruct((1, rows), jnp.flo...  148 us

profile of v2, /device:TPU:103, one launch (start us, length us, event | category | flops | bytes accessed | tf_op | source)
XLA Modules:
  0.0 151.0 jit_solution(8682222567848094748)
XLA Ops:
  0.6 147.7 %shard_map.50 = (f32[1,128]{1,0:T(1,128)}, f32[128,384]{1,0:T(8,128)}) custom-call(s32[1,128]{1,0:T(1,128)} %sel_ref.1, f32[1,3072,4,384]{3,2,1,0:T(4,128)} %w_hbm.1, f32[128,3072]{1,0:T(8,128)} %start_hbm.1), custom_call_target="tpu_custom_call" | custom-call | tf_op jit(solution)/shard_map/pallas_call | solution.py:237
  148.3 1.1 copy.7
  149.4 1.6 %copy.8 = f32[1,128,384]{2,1,0:T(8,128)} copy(f32[1,128,384]{2,1,0:T(8,128)} %bitcast.1) | data formatting | bytes 393216

commit v3 on v2

--- a/solution.py
+++ b/solution.py
@@ -11,9 +11,8 @@
 BATCH = 16
 FILL = 192
 SLOTS = 4
-SENDS = (0, 2, 1, 3)
-OWN, PASS, OTHER, PAIR = range(4)
-STEPS = ((0, OWN), (3, OWN), (0, OTHER), (2, OWN), (1, OWN), (3, OTHER), (2, OTHER), (1, OTHER))
+SENDS = ((2, 0), (0, 0), (1, 0), (3, 0))
+STEPS = ((0, 0), (2, 0), (3, 0), (1, 0), (0, 1), (2, 1), (3, 1), (1, 1))
 
 
 def kernel(
@@ -32,6 +31,7 @@
     following = lax.rem(section + 1, sections)
     before = lax.rem(section + sections - 1, sections)
     first, last = section == 0, section == sections - 1
+    passed = [ahead for ahead in range(chips) if ((chips - ahead) % chips, 1) not in SENDS]
 
     def fill(step, k):
         slot = lax.rem(step, SLOTS)
@@ -99,12 +99,13 @@
 
     def send(batch, index):
         at = rows_of(batch)
+        ahead, other = SENDS[index]
         return pltpu.make_async_remote_copy(
             src_ref=chosen_rows.at[at],
             dst_ref=left.at[at, block_of(me)],
             send_sem=send_sem.at[batch, index],
             recv_sem=recv_sem.at[batch, me],
-            device_id=(following, lax.rem(y + SENDS[index], chips) * 2 + core),
+            device_id=(following, lax.rem(y + ahead, chips) * 2 + (1 - core if other else core)),
             device_id_type=MESH,
         )
 
@@ -125,23 +126,19 @@
 
     lanes = lax.broadcasted_iota(jnp.int32, (BATCH, rows), 1)
 
-    def advance(batch, _):
+    def advance(fed, batch, _):
         at = rows_of(batch)
         square = jnp.zeros((BATCH, 128), jnp.float32)
         fresh = True
-        for ahead, what in STEPS:
+        for ahead, other in STEPS:
             chip = lax.rem(y + ahead, chips)
-            source = chip * 2 + (core if what in (OWN, PASS) else 1 - core)
-
-            @pl.when(jnp.logical_not(first))
-            def _():
+            source = chip * 2 + (1 - core if other else core)
+
+            if fed:
                 arrive(batch, source)
-                if what in (OWN, PASS):
+                if not other and ahead in passed:
                     relay(batch, source).start()
-
-            if what == PASS:
-                continue
-            span = block_of(chip * 2, 2) if what == PAIR else block_of(source)
+            span = block_of(source)
             x = left[at, span]
             high = x.astype(jnp.bfloat16).astype(jnp.float32)
             both = jnp.concatenate([high, x - high], axis=0).astype(jnp.bfloat16)
@@ -157,7 +154,7 @@
                 acc[...] += product
             fresh = False
         norm = jnp.sum(square, axis=1, keepdims=True) / width
-        scale = jnp.where(first, 1.0, 1.0 / jnp.sqrt(norm + 1e-06))
+        scale = 1.0 / jnp.sqrt(norm + 1e-06) if fed else 1.0
         chosen = jnp.zeros((BATCH, columns), jnp.float32)
         weight = jnp.zeros((BATCH, rows), jnp.float32)
         pick = picks[at, 0:1]
@@ -179,7 +176,13 @@
         part[at, :] = weight
         return 0
 
-    lax.fori_loop(0, batches, advance, 0)
+    @pl.when(first)
+    def _():
+        lax.fori_loop(0, batches, functools.partial(advance, False), 0)
+
+    @pl.when(jnp.logical_not(first))
+    def _():
+        lax.fori_loop(0, batches, functools.partial(advance, True), 0)
 
     totals[me] = part[...].T[:8]
 
@@ -221,8 +224,8 @@
 
         @pl.when(jnp.logical_not(first))
         def _():
-            for chip in range(peers // 2):
-                relay(batch, chip * 2 + core).wait_send()
+            for ahead in passed:
+                relay(batch, lax.rem(y + ahead, chips) * 2 + core).wait_send()
 
         return 0
 

time: 151 us -> 144 us (0.954)
  Pallas kernels: 148 us -> 140 us
    pallas_call x1, Pallas kernels: 148 us -> 140 us  [on_device(): pl.pallas_call(kernel, out_shape=(jax.ShapeDtypeStruct((1, rows), jnp.flo...]
where the time goes in v3:
time: 144 us
  Pallas kernels  140 us (97%)
  local copies, waits for them, and re-layouts  2.75 us (2%)
    pallas_call x1, Pallas kernels, on_device(): pl.pallas_call(kernel, out_shape=(jax.ShapeDtypeStruct((1, rows), jnp.flo...  140 us

profile of v3, /device:TPU:103, one launch (start us, length us, event | category | flops | bytes accessed | tf_op | source)
XLA Modules:
  0.0 143.8 jit_solution(12404616204873689403)
XLA Ops:
  0.6 140.4 %shard_map.50 = (f32[1,128]{1,0:T(1,128)}, f32[128,384]{1,0:T(8,128)}) custom-call(s32[1,128]{1,0:T(1,128)} %sel_ref.1, f32[1,3072,4,384]{3,2,1,0:T(4,128)} %w_hbm.1, f32[128,3072]{1,0:T(8,128)} %start_hbm.1), custom_call_target="tpu_custom_call" | custom-call | tf_op jit(solution)/shard_map/pallas_call | solution.py:240
  141.0 1.1 copy.7
  142.2 1.6 %copy.8 = f32[1,128,384]{2,1,0:T(8,128)} copy(f32[1,128,384]{2,1,0:T(8,128)} %bitcast.1) | data formatting | bytes 393216

commit v4 on v3

--- a/solution.py
+++ b/solution.py
@@ -9,15 +9,14 @@
 
 MESH = pl.DeviceIdType.MESH
 BATCH = 16
-FILL = 192
-SLOTS = 4
+SLOTS = 3
 SENDS = ((2, 0), (0, 0), (1, 0), (3, 0))
 STEPS = ((0, 0), (2, 0), (3, 0), (1, 0), (0, 1), (2, 1), (3, 1), (1, 1))
 
 
 def kernel(
-    sel_ref, w_hbm, start_hbm, prob_ref, rows_ref,
-    stage, whi, wlo, left, chosen_rows, acc, picks, part, totals, inverse,
+    sel_ref, w_hbm, start_hbm, sums_ref, raw_ref,
+    stage, whi, wlo, left, chosen_rows, acc, picks, part, totals,
     fill_sem, start_sem, send_sem, pass_sem, recv_sem, wsend_sem, wrecv_sem,
 ):
     rows, width = left.shape
@@ -25,7 +24,6 @@
     sections, peers = lax.axis_size("section"), lax.axis_size("bond")
     chips = peers // 2
     batches = rows // BATCH
-    fills = width // FILL
     section, me = lax.axis_index("section"), lax.axis_index("bond")
     y, core = me // 2, lax.rem(me, 2)
     following = lax.rem(section + 1, sections)
@@ -33,19 +31,19 @@
     first, last = section == 0, section == sections - 1
     passed = [ahead for ahead in range(chips) if ((chips - ahead) % chips, 1) not in SENDS]
 
+    @pl.when(first)
+    def _():
+        pltpu.make_async_copy(start_hbm, left, start_sem).start()
+
     def fill(step, k):
         slot = lax.rem(step, SLOTS)
         return pltpu.make_async_copy(
-            w_hbm.at[0, pl.ds(step * FILL, FILL), k, :], stage.at[slot, k], fill_sem.at[slot, k]
+            w_hbm.at[0, pl.ds(step * columns, columns), k, :], stage.at[slot, k], fill_sem.at[slot, k]
         )
 
     for step in range(SLOTS):
         for k in range(outcomes):
             fill(step, k).start()
-
-    @pl.when(first)
-    def _():
-        pltpu.make_async_copy(start_hbm, left, start_sem).start()
 
     barrier = pltpu.get_barrier_semaphore()
     for peer in range(peers):
@@ -58,6 +56,24 @@
 
     picks[...] = jnp.broadcast_to(sel_ref[...].astype(jnp.float32), (rows, rows)).T
 
+    def rows_of(batch):
+        return pl.ds(pl.multiple_of(batch * BATCH, BATCH), BATCH)
+
+    def block_of(source):
+        return pl.ds(pl.multiple_of(source * columns, columns), columns)
+
+    def multiply(x, span):
+        high = x.astype(jnp.bfloat16).astype(jnp.float32)
+        both = jnp.concatenate([high, x - high], axis=0).astype(jnp.bfloat16)
+        product = jnp.dot(both, whi[span, :], preferred_element_type=jnp.float32)
+        product = product[:BATCH] + product[BATCH:]
+        return product + jnp.dot(both[:BATCH], wlo[span, :], preferred_element_type=jnp.float32)
+
+    @pl.when(first)
+    def _():
+        pltpu.make_async_copy(start_hbm, left, start_sem).wait()
+        acc[...] = jnp.zeros_like(acc)
+
     def split(step, _):
         slot = lax.rem(step, SLOTS)
         for k in range(outcomes):
@@ -69,33 +85,27 @@
                 whole = stage[slot, k, pl.ds(row, 32), :]
                 high = whole.astype(jnp.bfloat16)
                 low = (whole - high.astype(jnp.float32)).astype(jnp.bfloat16)
-                at = pl.ds(pl.multiple_of(step * FILL + row, 32), 32)
+                at = pl.ds(pl.multiple_of(step * columns + row, 32), 32)
                 whi[at, k * columns : (k + 1) * columns] = high
                 wlo[at, k * columns : (k + 1) * columns] = low
             return 0
 
-        lax.fori_loop(0, FILL // 32, some, 0)
-
-        @pl.when(step + SLOTS < fills)
+        lax.fori_loop(0, columns // 32, some, 0)
+
+        @pl.when(step + SLOTS < peers)
         def _():
             for k in range(outcomes):
                 fill(step + SLOTS, k).start()
 
+        @pl.when(first)
+        def _():
+            acc[...] += multiply(left[rows_of(0), block_of(step)], block_of(step))
+
         return 0
 
-    lax.fori_loop(0, fills, split, 0)
+    lax.fori_loop(0, peers, split, 0)
 
     pl.semaphore_wait(barrier, 3 * peers - 1)
-
-    @pl.when(first)
-    def _():
-        pltpu.make_async_copy(start_hbm, left, start_sem).wait()
-
-    def rows_of(batch):
-        return pl.ds(pl.multiple_of(batch * BATCH, BATCH), BATCH)
-
-    def block_of(source, count=1):
-        return pl.ds(pl.multiple_of(source * columns, columns), count * columns)
 
     def send(batch, index):
         at = rows_of(batch)
@@ -126,11 +136,11 @@
 
     lanes = lax.broadcasted_iota(jnp.int32, (BATCH, rows), 1)
 
-    def advance(fed, batch, _):
+    def advance(fed, done, batch, _):
         at = rows_of(batch)
         square = jnp.zeros((BATCH, 128), jnp.float32)
         fresh = True
-        for ahead, other in STEPS:
+        for ahead, other in () if done else STEPS:
             chip = lax.rem(y + ahead, chips)
             source = chip * 2 + (1 - core if other else core)
 
@@ -140,14 +150,10 @@
                     relay(batch, source).start()
             span = block_of(source)
             x = left[at, span]
-            high = x.astype(jnp.bfloat16).astype(jnp.float32)
-            both = jnp.concatenate([high, x - high], axis=0).astype(jnp.bfloat16)
-            for lane in range(x.shape[1] // 128):
+            for lane in range(columns // 128):
                 piece = x[:, lane * 128 : (lane + 1) * 128]
                 square += piece * piece
-            product = jnp.dot(both, whi[span, :], preferred_element_type=jnp.float32)
-            product = product[:BATCH] + product[BATCH:]
-            product += jnp.dot(both[:BATCH], wlo[span, :], preferred_element_type=jnp.float32)
+            product = multiply(x, span)
             if fresh:
                 acc[...] = product
             else:
@@ -178,12 +184,15 @@
 
     @pl.when(first)
     def _():
-        lax.fori_loop(0, batches, functools.partial(advance, False), 0)
+        advance(False, True, 0, 0)
+        lax.fori_loop(1, batches, functools.partial(advance, False, False), 0)
 
     @pl.when(jnp.logical_not(first))
     def _():
-        lax.fori_loop(0, batches, functools.partial(advance, True), 0)
-
+        lax.fori_loop(0, batches, functools.partial(advance, True, False), 0)
+
+    result = pltpu.make_async_copy(chosen_rows, raw_ref, start_sem)
+    result.start()
     totals[me] = part[...].T[:8]
 
     def share(ahead):
@@ -208,10 +217,9 @@
     for k in range(outcomes):
         whole += total[k : k + 1]
         taken += jnp.where(sel_ref[...] == k, total[k : k + 1], 0.0)
-    prob_ref[...] = taken / whole
-    divisor = jnp.sqrt(taken / width + 1e-06)
-    inverse[...] = jnp.broadcast_to(divisor, (rows, rows)).T
-    rows_ref[...] = chosen_rows[...] / inverse[:, 0:1]
+    sums_ref[0:1] = taken
+    sums_ref[1:2] = whole
+    result.wait()
 
     for ahead in range(1, peers):
         share(ahead).wait_send()
@@ -230,6 +238,14 @@
         return 0
 
     lax.fori_loop(0, batches, drain, 0)
+
+
+def finish(width, sums_ref, raw_ref, prob_ref, rows_ref):
+    rows = raw_ref.shape[0]
+    taken = sums_ref[0:1]
+    prob_ref[...] = taken / sums_ref[1:2]
+    divisor = jnp.broadcast_to(jnp.sqrt(taken / width + 1e-06), (rows, rows)).T
+    rows_ref[0] = raw_ref[...] / divisor[:, 0:1]
 
 
 def on_device(site_tensor, boundary, selected):
@@ -237,10 +253,10 @@
     rows = boundary.shape[0]
     peers = lax.axis_size("bond")
     batches = rows // BATCH
-    prob, out = pl.pallas_call(
+    sums, raw = pl.pallas_call(
         kernel,
         out_shape=(
-            jax.ShapeDtypeStruct((1, rows), jnp.float32),
+            jax.ShapeDtypeStruct((2, rows), jnp.float32),
             jax.ShapeDtypeStruct((rows, columns), jnp.float32),
         ),
         in_specs=[
@@ -248,9 +264,9 @@
             pl.BlockSpec(memory_space=pl.ANY),
             pl.BlockSpec(memory_space=pl.ANY),
         ],
-        out_specs=(pl.BlockSpec(memory_space=pltpu.VMEM), pl.BlockSpec(memory_space=pltpu.VMEM)),
+        out_specs=(pl.BlockSpec(memory_space=pltpu.VMEM), pl.BlockSpec(memory_space=pl.ANY)),
         scratch_shapes=[
-            pltpu.VMEM((SLOTS, outcomes, FILL, columns), jnp.float32),
+            pltpu.VMEM((SLOTS, outcomes, columns, columns), jnp.float32),
             pltpu.VMEM((width, outcomes * columns), jnp.bfloat16),
             pltpu.VMEM((width, outcomes * columns), jnp.bfloat16),
             pltpu.VMEM((rows, width), jnp.float32),
@@ -259,7 +275,6 @@
             pltpu.VMEM((rows, rows), jnp.float32),
             pltpu.VMEM((rows, rows), jnp.float32),
             pltpu.VMEM((peers, 8, rows), jnp.float32),
-            pltpu.VMEM((rows, rows), jnp.float32),
             pltpu.SemaphoreType.DMA((SLOTS, outcomes)),
             pltpu.SemaphoreType.DMA,
             pltpu.SemaphoreType.DMA((batches, len(SENDS))),
@@ -272,7 +287,15 @@
             collective_id=0, has_side_effects=True, vmem_limit_bytes=60 * 2**20
         ),
     )(selected, site_tensor, boundary)
-    return prob, out[None]
+    return pl.pallas_call(
+        functools.partial(finish, width),
+        out_shape=(
+            jax.ShapeDtypeStruct((1, rows), jnp.float32),
+            jax.ShapeDtypeStruct((1, rows, columns), jnp.float32),
+        ),
+        in_specs=[pl.BlockSpec(memory_space=pltpu.VMEM)] * 2,
+        out_specs=(pl.BlockSpec(memory_space=pltpu.VMEM), pl.BlockSpec(memory_space=pltpu.VMEM)),
+    )(sums, raw)
 
 
 def solution(mesh):

time: 144 us -> 141 us (0.979)
  local copies, waits for them, and re-layouts: 2.75 us -> 0 us
    unnamed x2 -> x0, local copies, waits for them, and re-layouts: 2.75 us -> none
    pallas_call x1 -> x2, Pallas kernels: 140 us -> 140 us  [the longest x1 138 us: on_device(): pl.pallas_call(kernel, out_shape=(jax.ShapeDtypeStruct((2, rows), jnp.flo...]
where the time goes in v4:
time: 141 us
  Pallas kernels  140 us (99%)
    pallas_call x1, Pallas kernels, on_device(): pl.pallas_call(kernel, out_shape=(jax.ShapeDtypeStruct((2, rows), jnp.flo...  138 us

profile of v4, /device:TPU:103, one launch (start us, length us, event | category | flops | bytes accessed | tf_op | source)
XLA Modules:
  0.0 140.9 jit_solution(14052372502492257980)
XLA Ops:
  0.6 138.4 %shard_map.50 = (f32[2,128]{1,0:T(2,128)}, f32[128,384]{1,0:T(8,128)}) custom-call(s32[1,128]{1,0:T(1,128)} %sel_ref.1, f32[1,3072,4,384]{3,2,1,0:T(4,128)} %w_hbm.1, f32[128,3072]{1,0:T(8,128)} %start_hbm.1), custom_call_target="tpu_custom_call" | custom-call | tf_op jit(solution)/shard_map/pallas_call | solution.py:256
  139.1 1.8 %shard_map.51 = (f32[1,128]{1,0:T(1,128)}, f32[1,128,384]{2,1,0:T(8,128)}) custom-call(f32[2,128]{1,0:T(2,128)} %get-tuple-element.4.sums_ref, f32[128,384]{1,0:T(8,128)} %get-tuple-element.5.raw_ref), custom_call_target="tpu_custom_call" | custom-call | tf_op jit(solution)/shard_map/pallas_call | solution.py:290

commit v5 on v4

--- a/solution.py
+++ b/solution.py
@@ -56,6 +56,9 @@
 
     picks[...] = jnp.broadcast_to(sel_ref[...].astype(jnp.float32), (rows, rows)).T
 
+    def along(ahead, owner):
+        return lax.rem(y + ahead + owner * (2 * chips - 2 * ahead), chips)
+
     def rows_of(batch):
         return pl.ds(pl.multiple_of(batch * BATCH, BATCH), BATCH)
 
@@ -115,7 +118,7 @@
             dst_ref=left.at[at, block_of(me)],
             send_sem=send_sem.at[batch, index],
             recv_sem=recv_sem.at[batch, me],
-            device_id=(following, lax.rem(y + ahead, chips) * 2 + (1 - core if other else core)),
+            device_id=(following, along(ahead, core) * 2 + (1 - core if other else core)),
             device_id_type=MESH,
         )
 
@@ -141,8 +144,8 @@
         square = jnp.zeros((BATCH, 128), jnp.float32)
         fresh = True
         for ahead, other in () if done else STEPS:
-            chip = lax.rem(y + ahead, chips)
-            source = chip * 2 + (1 - core if other else core)
+            owner = 1 - core if other else core
+            source = along(ahead, owner) * 2 + owner
 
             if fed:
                 arrive(batch, source)

time: 141 us -> 141 us (level)
  no operation moved by 1% of the time
where the time goes in v5:
time: 141 us
  Pallas kernels  140 us (99%)
    pallas_call x1, Pallas kernels, on_device(): pl.pallas_call(kernel, out_shape=(jax.ShapeDtypeStruct((2, rows), jnp.flo...  138 us

profile of v5, /device:TPU:103, one launch (start us, length us, event | category | flops | bytes accessed | tf_op | source)
XLA Modules:
  0.0 140.7 jit_solution(10669436275011017911)
XLA Ops:
  0.6 138.3 %shard_map.50 = (f32[2,128]{1,0:T(2,128)}, f32[128,384]{1,0:T(8,128)}) custom-call(s32[1,128]{1,0:T(1,128)} %sel_ref.1, f32[1,3072,4,384]{3,2,1,0:T(4,128)} %w_hbm.1, f32[128,3072]{1,0:T(8,128)} %start_hbm.1), custom_call_target="tpu_custom_call" | custom-call | tf_op jit(solution)/shard_map/pallas_call | solution.py:259
  139.0 1.8 %shard_map.51 = (f32[1,128]{1,0:T(1,128)}, f32[1,128,384]{2,1,0:T(8,128)}) custom-call(f32[2,128]{1,0:T(2,128)} %get-tuple-element.4.sums_ref, f32[128,384]{1,0:T(8,128)} %get-tuple-element.5.raw_ref), custom_call_target="tpu_custom_call" | custom-call | tf_op jit(solution)/shard_map/pallas_call | solution.py:293
